TPU v7x, 256 devices: a whole 4x4x8 slice. The times are simulated.
256 devices in a mesh: row: 16 (over y, x), col: 16 (over z, core).
Axes of the slice: x: 4, y: 4, z: 8, core: 2. Of those that a mesh axis runs over, the one named last changes fastest.
Arguments:
- matrix: float32 [16384, 4, 4096], P('row', None, 'col'), may hold values from -28 to 28
Outputs:
- coefficients: float32 [512, 4, 4096], P(None, None, 'col')
- remainder: float32 [16384, 4, 4096], P('row', None, 'col')
All inputs are finite; a program needn't handle non-finite values.
Results may differ from a plain program's by a relative error of at most 0.0003.
Values sent between devices are 32-bit elements; how exact they have to be, the bound alone decides.
No kernel may reach another device: no remote copies, remote signals or barrier semaphores. Data moves between devices by JAX's collectives and lax.ppermute only.
A program may use at most 64 MiB of HBM per device.

v0:
```python
import jax
import jax.numpy as jnp
from jax import lax
from jax.sharding import PartitionSpec as P

BLOCK = 256
highest = lax.Precision.HIGHEST


def spread(block, axis, holder):
    block = jnp.where(lax.axis_index(axis) == holder, block, jnp.zeros_like(block))
    return lax.psum(block, axis)


def share_panel(work, owner):
    return spread(work[:, :BLOCK], "col", owner)


def reduce_rows(partial_value):
    return lax.psum(partial_value, "row")


def project_out(work, panel):
    gram = lax.dot_general(
        panel,
        panel,
        (((0,), (0,)), ((), ())),
        precision=highest,
        preferred_element_type=jnp.float32,
    )
    lower = jnp.linalg.cholesky(reduce_rows(gram))
    factor_t = jax.scipy.linalg.solve_triangular(lower, panel.T, lower=True)
    local_terms = jnp.dot(factor_t, work, precision=highest, preferred_element_type=jnp.float32)
    coeffs = lax.psum(local_terms, "row")
    update = lax.dot_general(
        factor_t,
        coeffs,
        (((0,), (0,)), ((), ())),
        precision=highest,
        preferred_element_type=jnp.float32,
    )
    return (work - update, coeffs)


def on_device(matrix):
    row_count, block_count, width = matrix.shape
    work = matrix.reshape(row_count, block_count * width)
    pieces = []
    for owner in range(2):
        panel = share_panel(work, owner)
        work, part_coeffs = project_out(work, panel)
        pieces.append(part_coeffs)
    coeffs = jnp.concatenate(pieces, axis=0)
    coefficients = coeffs.reshape(2 * BLOCK, block_count, width)
    return (coefficients, work.reshape(row_count, block_count, width))


def solution(mesh):
    return jax.shard_map(
        on_device,
        mesh=mesh,
        in_specs=(P("row", None, "col"),),
        out_specs=(P(None, None, "col"), P("row", None, "col")),
        check_vma=False,
    )
```

profile of v0, /device:TPU:32, one launch (start us, length us, event | category | flops | bytes accessed | tf_op | source)
XLA Modules:
  0.0 806.1 jit_solution(3339477113877099299)
XLA Ops:
  7.2 5.2 copy.3
  12.4 2.3 slice_select_fusion.1
  14.8 111.5 %all-reduce.8.cloned.1.call-done = f32[1024,256]{0,1:T(8,128)} async-done(((f32[1024,256]{0,1:T(8,128)}), f32[1024,256]{0,1:T(8,128)}) %all-reduce.8.cloned.1.call-update) | async-done | bytes 1048592 | tf_op jit(solution)/shard_map/psum | solution.py:12
  126.3 3.4 fusion.24
  129.8 98.0 %all-reduce.10.cloned.1.call-done = f32[256,256]{0,1:T(8,128)} async-done(((f32[256,256]{0,1:T(8,128)}), f32[256,256]{0,1:T(8,128)}) %all-reduce.10.cloned.1.call-update) | async-done | bytes 262160 | tf_op jit(solution)/shard_map/psum | solution.py:20
  229.8 11.7 %cholesky.130 = f32[128,128]{1,0:T(8,128)S(1)} custom-call(f32[128,128]{1,0:T(8,128)S(1)} %cholesky.194), custom_call_target="Cholesky" | custom-call | tf_op jit(solution)/shard_map/jit(cholesky)/cholesky | solution.py:31
  241.6 9.8 %custom-call.13 = f32[1,128,128]{1,2,0:T(8,128)S(1)} custom-call(f32[1,128,128]{2,1,0:T(8,128)S(1)} %get-tuple-element.49), custom_call_target="InvertDiagBlocksLowerTriangular" | custom-call | tf_op jit(solution)/shard_map/jit(cholesky)/cholesky | solution.py:31
  251.9 11.7 %cholesky.147 = f32[128,128]{1,0:T(8,128)S(1)} custom-call(f32[128,128]{1,0:T(8,128)S(1)} %convolution_subtract_fusion.5), custom_call_target="Cholesky" | custom-call | tf_op jit(solution)/shard_map/jit(cholesky)/cholesky | solution.py:31
  265.8 4.6 while.4
  266.9 1.4 bitcast_dynamic-update-slice_fusion.4
  269.0 1.4 bitcast_dynamic-update-slice_fusion.4
  270.4 19.7 %custom-call.14 = f32[2,128,128]{1,2,0:T(8,128)S(1)} custom-call(f32[2,128,128]{2,1,0:T(8,128)S(1)} %get-tuple-element.18), custom_call_target="InvertDiagBlocksLowerTriangular" | custom-call | tf_op jit(solution)/shard_map/jit(_solve_triangular)/triangular_solve | solution.py:32
  292.0 6.9 fusion.1
  298.9 96.7 %all-reduce.12.cloned.1.call-done = f32[256,1024]{1,0:T(8,128)} async-done(((f32[256,1024]{1,0:T(8,128)}), f32[256,1024]{1,0:T(8,128)}) %all-reduce.12.cloned.1.call-update) | async-done | bytes 1048592 | tf_op jit(solution)/shard_map/psum | solution.py:34
  395.6 7.2 convolution_subtract_fusion.1
  402.8 2.0 copy-done
  405.9 108.0 %all-reduce.14.cloned.1.call-done = f32[1024,256]{0,1:T(8,128)} async-done(((f32[1024,256]{0,1:T(8,128)}), f32[1024,256]{0,1:T(8,128)}) %all-reduce.14.cloned.1.call-update) | async-done | bytes 1048592 | tf_op jit(solution)/shard_map/psum | solution.py:12
  513.9 3.4 fusion.25
  517.5 97.6 %all-reduce.16.cloned.1.call-done = f32[256,256]{0,1:T(8,128)} async-done(((f32[256,256]{0,1:T(8,128)}), f32[256,256]{0,1:T(8,128)}) %all-reduce.16.cloned.1.call-update) | async-done | bytes 262160 | tf_op jit(solution)/shard_map/psum | solution.py:20
  617.2 11.7 %cholesky.164 = f32[128,128]{1,0:T(8,128)S(1)} custom-call(f32[128,128]{1,0:T(8,128)S(1)} %cholesky.197), custom_call_target="Cholesky" | custom-call | tf_op jit(solution)/shard_map/jit(cholesky)/cholesky | solution.py:31
  629.0 9.8 %custom-call.15 = f32[1,128,128]{1,2,0:T(8,128)S(1)} custom-call(f32[1,128,128]{2,1,0:T(8,128)S(1)} %get-tuple-element.45), custom_call_target="InvertDiagBlocksLowerTriangular" | custom-call | tf_op jit(solution)/shard_map/jit(cholesky)/cholesky | solution.py:31
  639.3 11.7 %cholesky.181 = f32[128,128]{1,0:T(8,128)S(1)} custom-call(f32[128,128]{1,0:T(8,128)S(1)} %convolution_subtract_fusion.4), custom_call_target="Cholesky" | custom-call | tf_op jit(solution)/shard_map/jit(cholesky)/cholesky | solution.py:31
  653.8 4.3 while.5
  654.6 1.4 bitcast_dynamic-update-slice_fusion.5
  656.7 1.4 bitcast_dynamic-update-slice_fusion.5
  658.1 19.7 %custom-call.16 = f32[2,128,128]{1,2,0:T(8,128)S(1)} custom-call(f32[2,128,128]{2,1,0:T(8,128)S(1)} %get-tuple-element.19), custom_call_target="InvertDiagBlocksLowerTriangular" | custom-call | tf_op jit(solution)/shard_map/jit(_solve_triangular)/triangular_solve | solution.py:32
  679.7 6.9 fusion
  686.5 96.8 %all-reduce.18.cloned.1.call-done = f32[256,1024]{1,0:T(8,128)} async-done(((f32[256,1024]{1,0:T(8,128)}), f32[256,1024]{1,0:T(8,128)}) %all-reduce.18.cloned.1.call-update) | async-done | bytes 1048592 | tf_op jit(solution)/shard_map/psum | solution.py:34
  783.3 7.0 convolution_subtract_fusion
  790.3 5.3 copy.8
  795.6 1.4 pad_maximum_fusion
  797.0 2.0 reshape.29
  (59 shorter events, 15.1 us)
Async XLA Ops:
  7.2 119.2 %all-reduce.8.cloned.1.call-start = ((), (), s32[]{:S(2)}) async-start(), calls=%async_computation | async-start | bytes 2097152 | tf_op jit(solution)/shard_map/psum | solution.py:12
  14.8 213.0 %all-reduce.10.cloned.1.call-start = ((), (), s32[]{:S(2)}) async-start(), calls=%async_computation.1 | async-start | bytes 524288 | tf_op jit(solution)/shard_map/psum | solution.py:20
  126.3 163.8 %copy-start.1 = (f32[1024,256]{0,1:T(8,128)S(1)}, f32[1024,256]{0,1:T(8,128)}, u32[]{:S(2)}) copy-start(f32[1024,256]{0,1:T(8,128)} %all-reduce.8.cloned.1.call-done) | copy-start | bytes 3145732
  129.7 265.9 %all-reduce.12.cloned.1.call-start = ((), (), s32[]{:S(2)}) async-start(), calls=%async_computation.2 | async-start | bytes 2097152 | tf_op jit(solution)/shard_map/psum | solution.py:34
  298.8 215.0 %all-reduce.14.cloned.1.call-start = ((), (), s32[]{:S(2)}) async-start(), calls=%async_computation.3 | async-start | bytes 2097152 | tf_op jit(solution)/shard_map/psum | solution.py:12
  402.8 2.0 copy-start
  405.9 209.3 %all-reduce.16.cloned.1.call-start = ((), (), s32[]{:S(2)}) async-start(), calls=%async_computation.4 | async-start | bytes 524288 | tf_op jit(solution)/shard_map/psum | solution.py:20
  513.9 163.9 %copy-start.2 = (f32[1024,256]{0,1:T(8,128)S(1)}, f32[1024,256]{0,1:T(8,128)}, u32[]{:S(2)}) copy-start(f32[1024,256]{0,1:T(8,128)} %all-reduce.14.cloned.1.call-done) | copy-start | bytes 3145732
  517.3 266.0 %all-reduce.18.cloned.1.call-start = ((), (), s32[]{:S(2)}) async-start(), calls=%async_computation.5 | async-start | bytes 2097152 | tf_op jit(solution)/shard_map/psum | solution.py:34
  790.3 5.3 copy-start.3
Sparse Core Ops, SparseCore 0:
  14.9 111.3 all-reduce.7
  130.4 97.2 all-reduce.9
  299.0 96.5 all-reduce.11
  406.0 107.8 all-reduce.13
  517.8 97.2 all-reduce.15
  686.7 96.5 all-reduce.17
where the time goes:
time: 815 us; the launch traced here: 806 us
  waiting for transfers between devices  609 us (75%)
  other arithmetic  115 us (14%)
  matrix products  39.2 us (5%)
  local copies, waits for them, and re-layouts  25 us (3%)
  between operations  17.3 us (2%)
    psum x2, waiting for transfers between devices, spread(): return lax.psum(block, axis)  219 us
    psum x2, waiting for transfers between devices, reduce_rows(): return lax.psum(partial_value, 'row')  196 us
    psum x2, waiting for transfers between devices, project_out(): coeffs = lax.psum(local_terms, 'row')  193 us
    another operation x13, other arithmetic, project_out(): lower = jnp.linalg.cholesky(reduce_rows(gram))  68.7 us
    another operation x5, other arithmetic, project_out(): factor_t = jax.scipy.linalg.solve_triangular(lower, panel.T, lower=True)  39.4 us
  transfers between devices with their start and end apart: 6, of which 6 were waited for; matrix products, arithmetic and copies ran while one was open for 0% of the time, Pallas kernels for 0%

commit v1 on v0

--- a/solution.py
+++ b/solution.py
@@ -5,6 +5,10 @@
 
 BLOCK = 256
 highest = lax.Precision.HIGHEST
+
+
+def domain_map(load):
+    return jnp.sum(jax.lax.all_gather(load, "row"), axis=0)
 
 
 def spread(block, axis, holder):
@@ -17,7 +21,7 @@
 
 
 def reduce_rows(partial_value):
-    return lax.psum(partial_value, "row")
+    return domain_map(partial_value)
 
 
 def project_out(work, panel):

time: 815 us -> 740 us (0.908)
  waiting for transfers between devices: 609 us -> 533 us
    psum x2 -> x0, waiting for transfers between devices: 196 us -> none  [reduce_rows(): return lax.psum(partial_value, 'row')]
    all_gather x0 -> x2, waiting for transfers between devices: none -> 119 us  [domain_map(): return jnp.sum(jax.lax.all_gather(load, 'row'), axis=0)]
where the time goes in v1:
time: 740 us; the launch traced here: 731 us
  waiting for transfers between devices  533 us (72%)
  other arithmetic  118 us (16%)
  matrix products  39.1 us (5%)
  local copies, waits for them, and re-layouts  22.9 us (3%)
  between operations  17.2 us (2%)
    psum x2, waiting for transfers between devices, spread(): return lax.psum(block, axis)  219 us
    psum x2, waiting for transfers between devices, project_out(): coeffs = lax.psum(local_terms, 'row')  194 us
    all_gather x2, waiting for transfers between devices, domain_map(): return jnp.sum(jax.lax.all_gather(load, 'row'), axis=0)  119 us
    another operation x13, other arithmetic, project_out(): lower = jnp.linalg.cholesky(reduce_rows(gram))  68.7 us
    another operation x5, other arithmetic, project_out(): factor_t = jax.scipy.linalg.solve_triangular(lower, panel.T, lower=True)  39.4 us
  transfers between devices with their start and end apart: 6, of which 6 were waited for; matrix products, arithmetic and copies ran while one was open for 0% of the time, Pallas kernels for 0%

profile of v1, /device:TPU:32, one launch (start us, length us, event | category | flops | bytes accessed | tf_op | source)
XLA Modules:
  0.0 731.2 jit_solution(16209530561162008839)
XLA Ops:
  7.2 5.2 copy.7
  12.4 2.3 slice_select_fusion.1
  14.8 111.5 %all-reduce.6.cloned.1.call-done = f32[1024,256]{0,1:T(8,128)} async-done(((f32[1024,256]{0,1:T(8,128)}), f32[1024,256]{0,1:T(8,128)}) %all-reduce.6.cloned.1.call-update) | async-done | bytes 1048592 | tf_op jit(solution)/shard_map/psum | solution.py:16
  126.3 3.3 fusion.24
  129.7 59.6 %all-gather.5.cloned.1.call-done = f32[4096,256]{1,0:T(8,128)} async-done(((f32[256,256]{1,0:T(8,128)}), f32[4096,256]{1,0:T(8,128)}) %all-gather.5.cloned.1.call-update) | async-done | bytes 4194320 | tf_op jit(solution)/shard_map/all_gather | solution.py:11
  189.3 2.6 reduce_sum.18
  192.1 11.7 %cholesky.130 = f32[128,128]{1,0:T(8,128)S(1)} custom-call(f32[128,128]{1,0:T(8,128)S(1)} %cholesky.194), custom_call_target="Cholesky" | custom-call | tf_op jit(solution)/shard_map/jit(cholesky)/cholesky | solution.py:35
  203.8 9.8 %custom-call.13 = f32[1,128,128]{1,2,0:T(8,128)S(1)} custom-call(f32[1,128,128]{2,1,0:T(8,128)S(1)} %get-tuple-element.51), custom_call_target="InvertDiagBlocksLowerTriangular" | custom-call | tf_op jit(solution)/shard_map/jit(cholesky)/cholesky | solution.py:35
  214.1 11.7 %cholesky.147 = f32[128,128]{1,0:T(8,128)S(1)} custom-call(f32[128,128]{1,0:T(8,128)S(1)} %convolution_subtract_fusion.5), custom_call_target="Cholesky" | custom-call | tf_op jit(solution)/shard_map/jit(cholesky)/cholesky | solution.py:35
  228.0 4.4 while.4
  232.4 19.7 %custom-call.14 = f32[2,128,128]{1,2,0:T(8,128)S(1)} custom-call(f32[2,128,128]{2,1,0:T(8,128)S(1)} %get-tuple-element.18), custom_call_target="InvertDiagBlocksLowerTriangular" | custom-call | tf_op jit(solution)/shard_map/jit(_solve_triangular)/triangular_solve | solution.py:36
  254.0 6.9 fusion.1
  260.9 97.0 %all-reduce.8.cloned.1.call-done = f32[256,1024]{1,0:T(8,128)} async-done(((f32[256,1024]{1,0:T(8,128)}), f32[256,1024]{1,0:T(8,128)}) %all-reduce.8.cloned.1.call-update) | async-done | bytes 1048592 | tf_op jit(solution)/shard_map/psum | solution.py:38
  358.0 7.2 convolution_subtract_fusion.1
  365.2 2.0 copy-done
  368.3 108.0 %all-reduce.10.cloned.1.call-done = f32[1024,256]{0,1:T(8,128)} async-done(((f32[1024,256]{0,1:T(8,128)}), f32[1024,256]{0,1:T(8,128)}) %all-reduce.10.cloned.1.call-update) | async-done | bytes 1048592 | tf_op jit(solution)/shard_map/psum | solution.py:16
  476.2 3.3 fusion.25
  479.8 59.4 %all-gather.7.cloned.1.call-done = f32[4096,256]{1,0:T(8,128)} async-done(((f32[256,256]{1,0:T(8,128)}), f32[4096,256]{1,0:T(8,128)}) %all-gather.7.cloned.1.call-update) | async-done | bytes 4194320 | tf_op jit(solution)/shard_map/all_gather | solution.py:11
  539.2 2.6 reduce_sum.19
  542.0 11.7 %cholesky.164 = f32[128,128]{1,0:T(8,128)S(1)} custom-call(f32[128,128]{1,0:T(8,128)S(1)} %cholesky.197), custom_call_target="Cholesky" | custom-call | tf_op jit(solution)/shard_map/jit(cholesky)/cholesky | solution.py:35
  553.8 9.8 %custom-call.15 = f32[1,128,128]{1,2,0:T(8,128)S(1)} custom-call(f32[1,128,128]{2,1,0:T(8,128)S(1)} %get-tuple-element.47), custom_call_target="InvertDiagBlocksLowerTriangular" | custom-call | tf_op jit(solution)/shard_map/jit(cholesky)/cholesky | solution.py:35
  564.1 11.7 %cholesky.181 = f32[128,128]{1,0:T(8,128)S(1)} custom-call(f32[128,128]{1,0:T(8,128)S(1)} %convolution_subtract_fusion.4), custom_call_target="Cholesky" | custom-call | tf_op jit(solution)/shard_map/jit(cholesky)/cholesky | solution.py:35
  578.6 4.3 while.5
  579.4 1.4 bitcast_dynamic-update-slice_fusion.5
  581.5 1.4 bitcast_dynamic-update-slice_fusion.5
  582.9 19.7 %custom-call.16 = f32[2,128,128]{1,2,0:T(8,128)S(1)} custom-call(f32[2,128,128]{2,1,0:T(8,128)S(1)} %get-tuple-element.19), custom_call_target="InvertDiagBlocksLowerTriangular" | custom-call | tf_op jit(solution)/shard_map/jit(_solve_triangular)/triangular_solve | solution.py:36
  604.5 6.9 fusion
  611.3 97.1 %all-reduce.12.cloned.1.call-done = f32[256,1024]{1,0:T(8,128)} async-done(((f32[256,1024]{1,0:T(8,128)}), f32[256,1024]{1,0:T(8,128)}) %all-reduce.12.cloned.1.call-update) | async-done | bytes 1048592 | tf_op jit(solution)/shard_map/psum | solution.py:38
  708.4 7.0 convolution_subtract_fusion
  715.4 5.3 copy.10
  720.7 1.4 pad_maximum_fusion
  722.1 2.0 reshape.29
  (61 shorter events, 14.1 us)
Async XLA Ops:
  7.2 119.2 %all-reduce.6.cloned.1.call-start = ((), (), s32[]{:S(2)}) async-start(), calls=%async_computation | async-start | bytes 2097152 | tf_op jit(solution)/shard_map/psum | solution.py:16
  14.8 174.5 %all-gather.5.cloned.1.call-start = ((), (), s32[]{:S(2)}) async-start(), calls=%async_computation.4 | async-start | bytes 4456448 | tf_op jit(solution)/shard_map/all_gather | solution.py:11
  129.6 228.3 %all-reduce.8.cloned.1.call-start = ((), (), s32[]{:S(2)}) async-start(), calls=%async_computation.1 | async-start | bytes 2097152 | tf_op jit(solution)/shard_map/psum | solution.py:38
  189.3 62.8 %copy-start.1 = (f32[1024,256]{0,1:T(8,128)S(1)}, f32[1024,256]{0,1:T(8,128)}, u32[]{:S(2)}) copy-start(f32[1024,256]{0,1:T(8,128)} %all-reduce.6.cloned.1.call-done) | copy-start | bytes 3145732
  260.9 215.4 %all-reduce.10.cloned.1.call-start = ((), (), s32[]{:S(2)}) async-start(), calls=%async_computation.2 | async-start | bytes 2097152 | tf_op jit(solution)/shard_map/psum | solution.py:16
  365.1 2.0 copy-start
  368.2 171.0 %all-gather.7.cloned.1.call-start = ((), (), s32[]{:S(2)}) async-start(), calls=%async_computation.5 | async-start | bytes 4456448 | tf_op jit(solution)/shard_map/all_gather | solution.py:11
  479.6 228.8 %all-reduce.12.cloned.1.call-start = ((), (), s32[]{:S(2)}) async-start(), calls=%async_computation.3 | async-start | bytes 2097152 | tf_op jit(solution)/shard_map/psum | solution.py:38
  539.2 63.3 %copy-start.2 = (f32[1024,256]{0,1:T(8,128)S(1)}, f32[1024,256]{0,1:T(8,128)}, u32[]{:S(2)}) copy-start(f32[1024,256]{0,1:T(8,128)} %all-reduce.10.cloned.1.call-done) | copy-start | bytes 3145732
  715.4 5.3 copy-start.3
Sparse Core Ops, SparseCore 0:
  14.9 111.3 all-reduce.5
  129.8 59.4 all-gather.4
  261.0 96.9 all-reduce.7
  368.4 107.8 all-reduce.9
  479.7 59.4 all-gather.6
  611.5 96.9 all-reduce.11
